TPU v7x, 512 devices: a whole 4x4x16 slice. The times are simulated.
512 devices in a mesh: island: 16 (over z), fsdp: 32 (over x, y, core).
Axes of the slice: x: 4, y: 4, z: 16, core: 2. Of those that a mesh axis runs over, the one named last changes fastest.
Arguments:
- activations: bfloat16 [16, 11776, 4096], P('island', 'fsdp'), may hold values from -6 to 6
- key_grad: bfloat16 [16, 11776, 512], P('island', 'fsdp'), may hold values from -0.0546875 to 0.0546875
- island_weight: float32 [16, 4096, 512], P('island', 'fsdp'), may hold values from -0.09375 to 0.09375
- adam_m: float32 [16, 4096, 512], P('island', 'fsdp'), may hold values from -6 to 6
- adam_v: float32 [16, 4096, 512], P('island', 'fsdp'), may hold values from 0.2 to 2
- anchor: float32 [16, 256, 512], P('island', 'fsdp'), may hold values from -0.09375 to 0.09375
- outer_momentum: float32 [16, 256, 512], P('island', 'fsdp'), may hold values from -0.09375 to 0.09375
Outputs:
- adam_m_next: float32 [16, 4096, 512], P('island', 'fsdp')
- adam_v_next: float32 [16, 4096, 512], P('island', 'fsdp')
- island_weight_next: float32 [4096, 512], P('fsdp')
- anchor_next: float32 [16, 256, 512], P('island', 'fsdp')
- momentum_next: float32 [16, 256, 512], P('island', 'fsdp')
All inputs are finite; a program needn't handle non-finite values.
Results may differ from a plain program's by a relative error of at most 0.0003.
Values may be sent and summed in bfloat16 or wider, within the bound.
A program may use at most 64 MiB of HBM per device.

v0:
```python
import jax
import jax.numpy as jnp
from jax import lax
from jax.sharding import PartitionSpec as P

beta_first = 0.9
beta_second = 0.95
epsilon = 1e-08
inner_rate = 0.0004
decay_rate = 0.1
outer_beta = 0.9
outer_rate = 0.7


def swapped(value, axis, bit):
    return lax.ppermute(value, axis, [(i, i ^ 1 << bit) for i in range(lax.axis_size(axis))])


def shards(activations, key_grad, island_weight, adam_m, adam_v, anchor, outer_momentum):
    inputs = activations[0]
    tangent = key_grad[0]
    row_count = island_weight.shape[1]
    columns = lax.all_to_all(inputs, "fsdp", split_axis=1, concat_axis=0, tiled=True)
    grad = lax.dot_general(
        columns,
        lax.all_gather(tangent, "fsdp", axis=0, tiled=True),
        (((0,), (0,)), ((), ())),
        preferred_element_type=jnp.float32,
    )
    m_next = beta_first * adam_m[0] + (1.0 - beta_first) * grad
    v_next = beta_second * adam_v[0] + (1.0 - beta_second) * grad * grad
    weight = island_weight[0]
    stepped = weight - inner_rate * (m_next / (jnp.sqrt(v_next) + epsilon) + decay_rate * weight)
    islands = lax.axis_size("island")
    levels = islands.bit_length() - 1
    share_rows = row_count // islands
    position = lax.axis_index("island")
    summed = stepped
    for bit in range(levels):
        summed = summed + swapped(summed, "island", bit)
    own_sum = lax.dynamic_slice_in_dim(summed, position * share_rows, share_rows, 0)
    anchor_block = anchor[0]
    shift = anchor_block - own_sum / float(islands)
    moment = outer_beta * outer_momentum[0] + shift
    new_anchor = anchor_block - outer_rate * (shift + outer_beta * moment)
    refreshed = lax.all_gather(new_anchor, "island", axis=0, tiled=True)
    return (m_next[None], v_next[None], refreshed, new_anchor[None], moment[None])


def solution(mesh):
    return jax.shard_map(
        shards,
        mesh=mesh,
        in_specs=(
            P("island", "fsdp", None),
            P("island", "fsdp", None),
            P("island", "fsdp", None),
            P("island", "fsdp", None),
            P("island", "fsdp", None),
            P("island", "fsdp", None),
            P("island", "fsdp", None),
        ),
        out_specs=(
            P("island", "fsdp", None),
            P("island", "fsdp", None),
            P("fsdp", None),
            P("island", "fsdp", None),
            P("island", "fsdp", None),
        ),
        check_vma=False,
    )
```

profile of v0, /device:TPU:2, one launch (start us, length us, event | category | flops | bytes accessed | tf_op | source)
XLA Modules:
  0.0 242.4 jit_solution(13812907711596420552)
XLA Ops:
  7.2 0.0 all-gather.3.cloned.1.call-start
  7.2 0.7 all-gather.3.cloned.1.call-update
  7.9 2.6 %copy.14 = bf16[46,8,32,128]{3,2,1,0:T(8,128)(2,1)S(1)} copy(bf16[46,8,32,128]{3,1,2,0:T(8,128)(2,1)} %bitcast.55) | data formatting | bytes 6029312
  10.5 1.2 copy.13
  11.7 0.0 copy-start
  11.7 0.0 copy-start.1
  11.7 50.5 %all_to_all.19 = bf16[368,32,128]{2,0,1:T(8,128)(2,1)S(1)} all-to-all(bf16[368,32,128]{2,0,1:T(8,128)(2,1)S(1)} %copy.13), channel_id=1, replica_groups=mesh['island'=16,'fsdp'=32] {'fsdp'}, dimensions={1} | all-to-all | bytes 6029312 | tf_op jit(solution)/shard_map/all_to_all | solution.py:23
  62.3 47.1 %all-gather.3.cloned.1.call-done = bf16[1,11776,512]{2,1,0:T(8,128)(2,1)} async-done(((bf16[1,368,512]{2,1,0:T(8,128)(2,1)}), bf16[1,11776,512]{2,1,0:T(8,128)(2,1)}) %all-gather.3.cloned.1.call-update) | async-done | bytes 12058640 | tf_op jit(solution)/shard_map/all_gather | solution.py:26
  109.4 0.0 copy-done
  109.4 0.0 copy-done.1
  109.4 0.0 copy-start.3
  109.4 7.1 %bitcast_subtract_fusion = (f32[128,512]{1,0:T(8,128)S(1)}, f32[1,128,512]{2,1,0:T(8,128)}, f32[1,128,512]{2,1,0:T(8,128)}) fusion(f32[1,128,512]{2,1,0:T(8,128)S(1)} %copy-done, f32[1,128,512]{2,1,0:T(8,128)S(1)} %copy-done.1, f32[1,128,512]{2,1,0:T(8,128)} %param.11, bf16[11776,128]{1,0:T(8,128)(2,1)S(1)} %bitcast.53, ...), kind=kOutput, calls=%fused_computation.4 | convolution fusion | flops 1544355840 | bytes 16646144 | tf_op jit(solution)/shard_map/dot_general | solution.py:24
  116.5 3.4 %collective-permute-start = (f32[128,512]{1,0:T(8,128)S(1)}, f32[128,512]{1,0:T(8,128)S(1)}, u32[]{:S(2)}, u32[]{:S(2)}) collective-permute-start(f32[128,512]{1,0:T(8,128)S(1)} %get-tuple-element.7), channel_id=1, source_target_pairs={{0,32},{32,0},{64,96},{96,64},{128,160},{160,128},{192,224},{224,1... | collective-permute-start | bytes 786440 | tf_op jit(solution)/shard_map/ppermute | solution.py:16
  120.0 6.9 %collective-permute-done = f32[128,512]{1,0:T(8,128)S(1)} collective-permute-done((f32[128,512]{1,0:T(8,128)S(1)}, f32[128,512]{1,0:T(8,128)S(1)}, u32[]{:S(2)}, u32[]{:S(2)}) %collective-permute-start) | collective-permute-done | bytes 262176 | tf_op jit(solution)/shard_map/ppermute | solution.py:16
  126.9 4.5 %collective-permute-start.1 = (f32[128,512]{1,0:T(8,128)S(1)}, f32[128,512]{1,0:T(8,128)S(1)}, u32[]{:S(2)}, u32[]{:S(2)}) collective-permute-start(f32[128,512]{1,0:T(8,128)S(1)} %add.41), channel_id=1, source_target_pairs={{0,64},{32,96},{64,0},{96,32},{128,192},{160,224},{192,128},{224,1... | collective-permute-start | bytes 786440 | tf_op jit(solution)/shard_map/ppermute | solution.py:16
  131.4 11.6 %collective-permute-done.1 = f32[128,512]{1,0:T(8,128)S(1)} collective-permute-done((f32[128,512]{1,0:T(8,128)S(1)}, f32[128,512]{1,0:T(8,128)S(1)}, u32[]{:S(2)}, u32[]{:S(2)}) %collective-permute-start.1) | collective-permute-done | bytes 262176 | tf_op jit(solution)/shard_map/ppermute | solution.py:16
  143.0 7.6 %collective-permute-start.2 = (f32[128,512]{1,0:T(8,128)S(1)}, f32[128,512]{1,0:T(8,128)S(1)}, u32[]{:S(2)}, u32[]{:S(2)}) collective-permute-start(f32[128,512]{1,0:T(8,128)S(1)} %add.42), channel_id=1, source_target_pairs={{0,128},{32,160},{64,192},{96,224},{128,0},{160,32},{192,64},{224,... | collective-permute-start | bytes 786440 | tf_op jit(solution)/shard_map/ppermute | solution.py:16
  150.7 21.2 %collective-permute-done.2 = f32[128,512]{1,0:T(8,128)S(1)} collective-permute-done((f32[128,512]{1,0:T(8,128)S(1)}, f32[128,512]{1,0:T(8,128)S(1)}, u32[]{:S(2)}, u32[]{:S(2)}) %collective-permute-start.2) | collective-permute-done | bytes 262176 | tf_op jit(solution)/shard_map/ppermute | solution.py:16
  171.9 11.5 %collective-permute-start.3 = (f32[128,512]{1,0:T(8,128)S(1)}, f32[128,512]{1,0:T(8,128)S(1)}, u32[]{:S(2)}, u32[]{:S(2)}) collective-permute-start(f32[128,512]{1,0:T(8,128)S(1)} %add.43), channel_id=1, source_target_pairs={{0,256},{32,288},{64,320},{96,352},{128,384},{160,416},{192,448},{... | collective-permute-start | bytes 786440 | tf_op jit(solution)/shard_map/ppermute | solution.py:16
  183.4 22.2 %collective-permute-done.3 = f32[128,512]{1,0:T(8,128)S(1)} collective-permute-done((f32[128,512]{1,0:T(8,128)S(1)}, f32[128,512]{1,0:T(8,128)S(1)}, u32[]{:S(2)}, u32[]{:S(2)}) %collective-permute-start.3) | collective-permute-done | bytes 262176 | tf_op jit(solution)/shard_map/ppermute | solution.py:16
  205.6 0.0 copy-done.3
  205.6 1.3 fusion.9
  207.0 0.0 copy-start.2
  207.0 27.9 %all_gather.7 = f32[128,512]{1,0:T(8,128)S(1)} all-gather(f32[8,512]{1,0:T(8,128)S(1)} %get-tuple-element.6), channel_id=1, replica_groups=mesh['island'=16,'fsdp'=32] {'island'}, dimensions={0}, use_global_device_ids=true | all-gather | bytes 278528 | tf_op jit(solution)/shard_map/all_gather | solution.py:46
  234.9 0.7 copy.16
  235.6 0.0 copy-done.2
  (3 shorter events, 0.1 us)
Async XLA Ops:
  7.2 102.2 %all-gather.3.cloned.1.call-start = ((), (), s32[]{:S(2)}) async-start(), calls=%async_computation.1 | async-start | bytes 12435456 | tf_op jit(solution)/shard_map/all_gather | solution.py:26
  11.7 97.6 %copy-start = (f32[1,128,512]{2,1,0:T(8,128)S(1)}, f32[1,128,512]{2,1,0:T(8,128)}, u32[]{:S(2)}) copy-start(f32[1,128,512]{2,1,0:T(8,128)} %param.9) | copy-start | bytes 786436
  11.7 97.6 %copy-start.1 = (f32[1,128,512]{2,1,0:T(8,128)S(1)}, f32[1,128,512]{2,1,0:T(8,128)}, u32[]{:S(2)}) copy-start(f32[1,128,512]{2,1,0:T(8,128)} %param.10) | copy-start | bytes 786436
  109.4 96.3 %copy-start.3 = (f32[1,8,512]{2,1,0:T(8,128)S(1)}, f32[1,8,512]{2,1,0:T(8,128)}, u32[]{:S(2)}) copy-start(f32[1,8,512]{2,1,0:T(8,128)} %param.13) | copy-start | bytes 49156
  116.5 10.3 %collective-permute-start = (f32[128,512]{1,0:T(8,128)S(1)}, f32[128,512]{1,0:T(8,128)S(1)}, u32[]{:S(2)}, u32[]{:S(2)}) collective-permute-start(f32[128,512]{1,0:T(8,128)S(1)} %get-tuple-element.7), channel_id=1, source_target_pairs={{0,32},{32,0},{64,96},{96,64},{128,160},{160,128},{192,224},{224,1... | collective-permute-start | bytes 786440 | tf_op jit(solution)/shard_map/ppermute | solution.py:16
  126.9 16.1 %collective-permute-start.1 = (f32[128,512]{1,0:T(8,128)S(1)}, f32[128,512]{1,0:T(8,128)S(1)}, u32[]{:S(2)}, u32[]{:S(2)}) collective-permute-start(f32[128,512]{1,0:T(8,128)S(1)} %add.41), channel_id=1, source_target_pairs={{0,64},{32,96},{64,0},{96,32},{128,192},{160,224},{192,128},{224,1... | collective-permute-start | bytes 786440 | tf_op jit(solution)/shard_map/ppermute | solution.py:16
  143.0 28.9 %collective-permute-start.2 = (f32[128,512]{1,0:T(8,128)S(1)}, f32[128,512]{1,0:T(8,128)S(1)}, u32[]{:S(2)}, u32[]{:S(2)}) collective-permute-start(f32[128,512]{1,0:T(8,128)S(1)} %add.42), channel_id=1, source_target_pairs={{0,128},{32,160},{64,192},{96,224},{128,0},{160,32},{192,64},{224,... | collective-permute-start | bytes 786440 | tf_op jit(solution)/shard_map/ppermute | solution.py:16
  171.9 33.7 %collective-permute-start.3 = (f32[128,512]{1,0:T(8,128)S(1)}, f32[128,512]{1,0:T(8,128)S(1)}, u32[]{:S(2)}, u32[]{:S(2)}) collective-permute-start(f32[128,512]{1,0:T(8,128)S(1)} %add.43), channel_id=1, source_target_pairs={{0,256},{32,288},{64,320},{96,352},{128,384},{160,416},{192,448},{... | collective-permute-start | bytes 786440 | tf_op jit(solution)/shard_map/ppermute | solution.py:16
  207.0 28.6 %copy-start.2 = (f32[8,512]{1,0:T(8,128)}, f32[8,512]{1,0:T(8,128)S(1)}, u32[]{:S(2)}) copy-start(f32[8,512]{1,0:T(8,128)S(1)} %get-tuple-element.6) | copy-start | bytes 49156
Sparse Core Ops, SparseCore 0:
  11.1 98.1 all-gather.2
where the time goes:
time: 243 us; the launch traced here: 242 us
  waiting for transfers between devices  110 us (45%)
  blocking collectives  78.4 us (32%)
  starting transfers between devices  27.1 us (11%)
  between operations  14.1 us (6%)
  matrix products  7.15 us (3%)
  local copies, waits for them, and re-layouts  4.52 us (2%)
    ppermute x4, waiting for transfers between devices, swapped(): lax.ppermute(value, axis, [(i, i ^ 1 << bit) for i in range(lax.axis_size...  61.9 us
    all_to_all x1, blocking collectives, shards(): lax.all_to_all(inputs, 'fsdp', split_axis=1, concat_axis=0, tiled=True)  50.5 us
    all_gather x1, waiting for transfers between devices, shards(): lax.all_gather(tangent, 'fsdp', axis=0, tiled=True)  47.1 us
    all_gather x1, blocking collectives, shards(): refreshed = lax.all_gather(new_anchor, 'island', axis=0, tiled=True)  27.9 us
    ppermute x4, starting transfers between devices, swapped(): lax.ppermute(value, axis, [(i, i ^ 1 << bit) for i in range(lax.axis_size...  27.1 us
    dot_general x1, matrix products, shards(): lax.dot_general(columns, lax.all_gather(tangent, 'fsdp', axis=0, tiled=Tr...  7.15 us
  transfers between devices with their start and end apart: 5, of which 5 were waited for; matrix products, arithmetic and copies ran while one was open for 2% of the time, Pallas kernels for 0%

commit v1 on v0

v1 whole, which is shorter than its diff:
```python
import jax
import jax.numpy as jnp
from jax import lax
from jax.experimental import pallas as pl
from jax.experimental.pallas import tpu as pltpu
from jax.sharding import PartitionSpec as P

beta_first = 0.9
beta_second = 0.95
epsilon = 1e-08
inner_rate = 0.0004
decay_rate = 0.1
outer_beta = 0.9
outer_rate = 0.7

SIDE = 4
STAGES = 4
MESH = pl.DeviceIdType.MESH


def window(
    islands,
    act, kg, weight, adam_m, adam_v, anchor, momentum,
    m_out, v_out, w_out, a_out, o_out,
    actb, kgb, part, got1, got2, wb, mb, vb, mnb, vnb, step_b, zgot, ab, ob, anb, onb,
    load_sem, act_sem, sib_send, sib_recv, xy_send, xy_recv, zr_send, zr_recv, ag_send, ag_recv, out_sem,
):
    me = lax.axis_index("island")
    flat = lax.axis_index("fsdp")
    core = lax.rem(flat, 2)
    chip = lax.div(flat, 2)
    x = lax.div(chip, SIDE)
    y = lax.rem(chip, SIDE)
    tokens = kg.shape[0]
    groups = islands // STAGES
    half_cols = kgb.shape[1] // 2
    sibling = flat + 1 - 2 * core

    def wrap(p):
        return lax.rem(p + 2 * SIDE, SIDE)

    def device(px, py):
        return (px * SIDE + py) * 2 + core

    loads = [
        pltpu.make_async_copy(kg, kgb.at[pl.ds(0, tokens)], load_sem.at[0]),
        pltpu.make_async_copy(weight, wb, load_sem.at[1]),
        pltpu.make_async_copy(adam_m, mb, load_sem.at[2]),
        pltpu.make_async_copy(adam_v, vb, load_sem.at[3]),
        pltpu.make_async_copy(anchor, ab, load_sem.at[4]),
        pltpu.make_async_copy(momentum, ob, load_sem.at[5]),
    ]

    def own_block(k):
        start = pl.multiple_of((2 * k + core) * 128, 128)
        return pltpu.make_async_copy(
            act.at[:, pl.ds(start, 128)], actb.at[k, pl.ds(0, tokens)], act_sem.at[k]
        )

    def sibling_block(k):
        start = pl.multiple_of((2 * k + 1 - core) * 128, 128)
        return pltpu.make_async_remote_copy(
            src_ref=act.at[:, pl.ds(start, 128)],
            dst_ref=actb.at[k, pl.ds(tokens, tokens)],
            send_sem=sib_send.at[k],
            recv_sem=sib_recv.at[k],
            device_id={"fsdp": sibling},
            device_id_type=MESH,
        )

    sibling_kg = pltpu.make_async_remote_copy(
        src_ref=kg,
        dst_ref=kgb.at[pl.ds(tokens, tokens)],
        send_sem=sib_send.at[SIDE * SIDE],
        recv_sem=sib_recv.at[SIDE * SIDE],
        device_id={"fsdp": sibling},
        device_id_type=MESH,
    )

    def far_x(visit):
        def one(e, carry):
            visit(wrap(x + 2) * SIDE + e)
            return carry

        lax.fori_loop(0, SIDE, one, 0)

    def far_y(visit):
        def one(e, carry):
            visit(wrap(x + 3 + e) * SIDE + wrap(y + 2))
            return carry

        lax.fori_loop(0, SIDE - 1, one, 0)

    def rest(visit):
        def one(e, carry):
            visit(wrap(x + 3 + lax.div(e, 3)) * SIDE + wrap(y + 3 + lax.rem(e, 3)))
            return carry

        lax.fori_loop(0, 9, one, 0)

    loads[0].start()
    for visits in (far_x, far_y, rest):
        visits(lambda k: own_block(k).start())
    for copy in loads[1:]:
        copy.start()

    barrier = pltpu.get_barrier_semaphore()
    for peer in (
        sibling,
        device(wrap(x + 1), y),
        device(wrap(x - 1), y),
        device(x, wrap(y + 1)),
        device(x, wrap(y - 1)),
    ):
        pl.semaphore_signal(barrier, inc=1, device_id={"fsdp": peer}, device_id_type=MESH)

    def greet(d, carry):
        pl.semaphore_signal(
            barrier, inc=1, device_id={"island": lax.rem(me + d, islands)}, device_id_type=MESH
        )
        return carry

    lax.fori_loop(1, islands, greet, 0)
    pl.semaphore_wait(barrier, 5 + islands - 1)

    sibling_kg.start()
    for visits in (far_x, far_y, rest):
        visits(lambda k: sibling_block(k).start())

    def neighbour(axis, direction):
        sign = 1 - 2 * direction
        if axis == 0:
            return device(wrap(x + sign), y)
        return device(x, wrap(y + sign))

    def axis_of(phase, half):
        return phase ^ half

    def position(axis):
        return x if axis == 0 else y

    def piece(s, phase, half, group, section):
        if phase == 0:
            return part.at[s, half, pl.ds(group * SIDE + 2 * section, 2)]
        own = position(axis_of(0, half))
        rows = part.shape[3] // 2
        return part.at[s, half, own * SIDE + group, pl.ds(rows * section, rows)]

    def landing(s, phase, half, direction, message):
        buffer = got1 if phase == 0 else got2
        return buffer.at[s, half, direction, message]

    def send(s, phase, half, direction, message):
        axis = axis_of(phase, half)
        pos = position(axis)
        sign = 1 - 2 * direction
        group = wrap(pos + 2) if message == 0 else wrap(pos + sign)
        section = 1 - direction if message == 1 else direction
        return pltpu.make_async_remote_copy(
            src_ref=piece(s, phase, half, group, section),
            dst_ref=landing(s, phase, half, direction, message),
            send_sem=xy_send.at[s, phase, half, direction, message],
            recv_sem=xy_recv.at[s, phase, half, direction, message],
            device_id={"fsdp": neighbour(axis, direction)},
            device_id_type=MESH,
        )

    def first(s, phase, half):
        for direction in (0, 1):
            send(s, phase, half, direction, 0).start()

    def second(s, phase, half):
        for direction in (0, 1):
            send(s, phase, half, direction, 1).start()

    def relay(s, phase, half):
        pos = position(axis_of(phase, half))
        for direction in (0, 1):
            send(s, phase, half, direction, 0).wait_recv()
            target = piece(s, phase, half, wrap(pos + 1 - 2 * direction), direction)
            target[...] += landing(s, phase, half, direction, 0)[...]
            send(s, phase, half, direction, 2).start()

    def arrived(s, phase, half):
        for direction in (0, 1):
            for message in (1, 2):
                send(s, phase, half, direction, message).wait_recv()

    def collect(s, phase, half):
        arrived(s, phase, half)
        pos = position(axis_of(phase, half))
        for section in (0, 1):
            target = piece(s, phase, half, pos, section)
            target[...] += (
                landing(s, phase, half, section, 2)[...]
                + landing(s, phase, half, 1 - section, 1)[...]
            )

    def share_send(s, j):
        owner = STAGES * j + s
        return pltpu.make_async_remote_copy(
            src_ref=step_b.at[s, j],
            dst_ref=zgot.at[me],
            send_sem=zr_send.at[owner],
            recv_sem=zr_recv.at[me],
            device_id={"island": owner},
            device_id_type=MESH,
        )

    def share_from(source):
        return pltpu.make_async_remote_copy(
            src_ref=step_b.at[0, 0],
            dst_ref=zgot.at[source],
            send_sem=zr_send.at[source],
            recv_sem=zr_recv.at[source],
            device_id={"island": source},
            device_id_type=MESH,
        )

    def fresh_send(owner, target):
        return pltpu.make_async_remote_copy(
            src_ref=anb,
            dst_ref=w_out.at[owner],
            send_sem=ag_send.at[target],
            recv_sem=ag_recv.at[owner],
            device_id={"island": target},
            device_id_type=MESH,
        )

    def save_moments(s):
        return (
            pltpu.make_async_copy(mnb.at[:, s], m_out.at[:, s], out_sem.at[0, s]),
            pltpu.make_async_copy(vnb.at[:, s], v_out.at[:, s], out_sem.at[1, s]),
        )

    save_outer = (
        pltpu.make_async_copy(anb, a_out, out_sem.at[2, 0]),
        pltpu.make_async_copy(onb, o_out, out_sem.at[2, 1]),
        pltpu.make_async_copy(anb, w_out.at[me], out_sem.at[2, 2]),
    )

    def inner_step(s):
        for half in (0, 1):
            arrived(s, 1, half)
            pos = position(axis_of(1, half))
            cols = slice(half * half_cols, (half + 1) * half_cols)
            for section in (0, 1):
                js = slice(section * groups // 2, (section + 1) * groups // 2)
                shape = (groups // 2, 8, half_cols)
                grad = (
                    piece(s, 1, half, pos, section)[...]
                    + landing(s, 1, half, section, 2)[...]
                    + landing(s, 1, half, 1 - section, 1)[...]
                ).reshape(shape)
                m_next = beta_first * mb[js, s, :, cols] + (1.0 - beta_first) * grad
                v_next = beta_second * vb[js, s, :, cols] + (1.0 - beta_second) * grad * grad
                old = wb[js, s, :, cols]
                mnb[js, s, :, cols] = m_next
                vnb[js, s, :, cols] = v_next
                step_b[s, js, :, cols] = old - inner_rate * (
                    m_next / (jnp.sqrt(v_next) + epsilon) + decay_rate * old
                )
        for copy in save_moments(s):
            copy.start()

        def one(j, carry):
            @pl.when(STAGES * j + s != me)
            def _():
                share_send(s, j).start()

            return carry

        lax.fori_loop(0, groups, one, 0)

    def outer_step(s):
        @pl.when(lax.rem(me, STAGES) == s)
        def _():
            def add(d, total):
                source = lax.rem(me + d, islands)
                share_from(source).wait_recv()
                return total + zgot[source]

            total = lax.fori_loop(1, islands, add, step_b[s, lax.div(me, STAGES)])
            shift = ab[...] - total / float(islands)
            moment = outer_beta * ob[...] + shift
            anb[...] = ab[...] - outer_rate * (shift + outer_beta * moment)
            onb[...] = moment

            def one(d, carry):
                fresh_send(me, lax.rem(me + d, islands)).start()
                return carry

            lax.fori_loop(1, islands, one, 0)
            for copy in save_outer:
                copy.start()

    def wait_block(k):
        own_block(k).wait()
        sibling_block(k).wait_recv()

    def multiply(half, offset):
        axis = axis_of(0, half)
        group = wrap(position(axis) + offset)

        def one(e, carry):
            k = group * SIDE + e if half == 0 else e * SIDE + group
            product = lax.dot_general(
                actb[k],
                kgb[:, half * half_cols : (half + 1) * half_cols],
                (((0,), (0,)), ((), ())),
                preferred_element_type=jnp.float32,
            )
            for s in range(STAGES):
                for j in range(groups):
                    row = (j * STAGES + s) * 8
                    part[s, half, group * SIDE + e, j * 8 : (j + 1) * 8, :] = product[row : row + 8, :]
            return carry

        lax.fori_loop(0, SIDE, one, 0)

    loads[0].wait()
    sibling_kg.wait_recv()
    far_x(wait_block)
    multiply(0, 2)
    first(0, 0, 0)
    far_y(wait_block)
    multiply(1, 2)
    first(0, 0, 1)
    rest(wait_block)
    for half in (0, 1):
        multiply(half, 1)
        send(0, 0, half, 0, 1).start()
    for half in (0, 1):
        multiply(half, 3)
        send(0, 0, half, 1, 1).start()
    for half in (0, 1):
        multiply(half, 0)
    for copy in loads[1:]:
        copy.wait()

    def stage(t, carry):
        @pl.when(t < STAGES)
        def _():
            for half in (0, 1):
                relay(t, 0, half)

        @pl.when(t + 1 < STAGES)
        def _():
            for half in (0, 1):
                first(t + 1, 0, half)

        @pl.when(t >= 1)
        def _():
            inner_step(t - 1)

        @pl.when(t < STAGES)
        def _():
            for half in (0, 1):
                collect(t, 0, half)
                first(t, 1, half)
                second(t, 1, half)

        @pl.when(t + 1 < STAGES)
        def _():
            for half in (0, 1):
                second(t + 1, 0, half)

        @pl.when(t < STAGES)
        def _():
            for half in (0, 1):
                relay(t, 1, half)

        @pl.when(t >= 1)
        def _():
            outer_step(t - 1)

        return carry

    lax.fori_loop(0, STAGES + 1, stage, 0)

    sibling_kg.wait_send()
    for visits in (far_x, far_y, rest):
        visits(lambda k: sibling_block(k).wait_send())

    def finish(s, carry):
        for phase in (0, 1):
            for half in (0, 1):
                for direction in (0, 1):
                    for message in (0, 1, 2):
                        send(s, phase, half, direction, message).wait_send()
        for copy in save_moments(s):
            copy.wait()
        return carry

    lax.fori_loop(0, STAGES, finish, 0)

    def last(d, carry):
        other = lax.rem(me + d, islands)
        fresh_send(other, me).wait_recv()
        share_from(other).wait_send()
        fresh_send(me, other).wait_send()
        return carry

    lax.fori_loop(1, islands, last, 0)
    for copy in save_outer:
        copy.wait()


def shards(activations, key_grad, island_weight, adam_m, adam_v, anchor, outer_momentum):
    _, tokens, features = activations.shape
    columns = key_grad.shape[2]
    rows = island_weight.shape[1]
    islands = lax.axis_size("island")
    groups = islands // STAGES
    share = rows // islands
    half_cols = columns // 2
    blocks = SIDE * SIDE
    f32 = jnp.float32
    state = (groups, STAGES, share, columns)
    hbm = pl.BlockSpec(memory_space=pl.ANY)
    dma = pltpu.SemaphoreType.DMA
    stage_rows = rows // STAGES

    def kernel(*refs):
        window(islands, *refs)

    m_next, v_next, refreshed, new_anchor, moment = pl.pallas_call(
        kernel,
        out_shape=(
            jax.ShapeDtypeStruct(state, f32),
            jax.ShapeDtypeStruct(state, f32),
            jax.ShapeDtypeStruct((islands, share, columns), f32),
            jax.ShapeDtypeStruct((share, columns), f32),
            jax.ShapeDtypeStruct((share, columns), f32),
        ),
        in_specs=[hbm] * 7,
        out_specs=(hbm,) * 5,
        scratch_shapes=[
            pltpu.VMEM((blocks, 2 * tokens, features // (2 * blocks)), jnp.bfloat16),
            pltpu.VMEM((2 * tokens, columns), jnp.bfloat16),
            pltpu.VMEM((STAGES, 2, blocks, stage_rows, half_cols), f32),
            pltpu.VMEM((STAGES, 2, 2, 3, 2, stage_rows, half_cols), f32),
            pltpu.VMEM((STAGES, 2, 2, 3, stage_rows // 2, half_cols), f32),
            pltpu.VMEM(state, f32),
            pltpu.VMEM(state, f32),
            pltpu.VMEM(state, f32),
            pltpu.VMEM(state, f32),
            pltpu.VMEM(state, f32),
            pltpu.VMEM((STAGES, groups, share, columns), f32),
            pltpu.VMEM((islands, share, columns), f32),
            pltpu.VMEM((share, columns), f32),
            pltpu.VMEM((share, columns), f32),
            pltpu.VMEM((share, columns), f32),
            pltpu.VMEM((share, columns), f32),
            dma((6,)),
            dma((blocks,)),
            dma((blocks + 1,)),
            dma((blocks + 1,)),
            dma((STAGES, 2, 2, 2, 3)),
            dma((STAGES, 2, 2, 2, 3)),
            dma((islands,)),
            dma((islands,)),
            dma((islands,)),
            dma((islands,)),
            dma((3, STAGES)),
        ],
        compiler_params=pltpu.CompilerParams(
            collective_id=0, has_side_effects=True, vmem_limit_bytes=48 * 1024 * 1024
        ),
    )(
        activations[0],
        key_grad[0],
        island_weight.reshape(state),
        adam_m.reshape(state),
        adam_v.reshape(state),
        anchor[0],
        outer_momentum[0],
    )
    return (
        m_next.reshape(island_weight.shape),
        v_next.reshape(island_weight.shape),
        refreshed.reshape(rows, columns),
        new_anchor[None],
        moment[None],
    )


def solution(mesh):
    spec = P("island", "fsdp", None)
    return jax.shard_map(
        shards,
        mesh=mesh,
        in_specs=(spec,) * 7,
        out_specs=(spec, spec, P("fsdp", None), spec, spec),
        check_vma=False,
    )
```

time: 243 us -> 98.8 us (0.41)
  the two profiles are of different devices: /device:TPU:2 before, /device:TPU:8 now
where the time goes in v1:
time: 98.8 us; the launch traced here: 98.4 us
  Pallas kernels  87.3 us (88%)
  local copies, waits for them, and re-layouts  10.4 us (11%)
    pallas_call x1, Pallas kernels, shards(): pl.pallas_call(kernel, out_shape=(jax.ShapeDtypeStruct(state, f32), jax.S...  87.3 us
    unnamed x19, local copies, waits for them, and re-layouts  10.4 us

profile of v1, /device:TPU:8, one launch (start us, length us, event | category | flops | bytes accessed | tf_op | source)
XLA Modules:
  0.0 98.4 jit_solution(7127230166996568231)
XLA Ops:
  0.6 0.0 copy-start
  0.6 1.8 %copy-done = bf16[1,368,4096]{2,1,0:T(8,128)(2,1)S(1)} copy-done((bf16[1,368,4096]{2,1,0:T(8,128)(2,1)S(1)}, bf16[1,368,4096]{2,1,0:T(8,128)(2,1)}, u32[]{:S(2)}) %copy-start) | copy-done | bytes 3014680
  2.5 0.0 copy-start.1
  2.5 1.0 %copy-done.1 = bf16[1,368,512]{2,1,0:T(8,128)(2,1)S(1)} copy-done((bf16[1,368,512]{2,1,0:T(8,128)(2,1)S(1)}, bf16[1,368,512]{2,1,0:T(8,128)(2,1)}, u32[]{:S(2)}) %copy-start.1) | copy-done | bytes 376856
  3.5 0.0 copy-start.2
  3.5 0.9 copy-done.2
  4.4 0.0 copy-start.3
  4.4 0.9 copy-done.3
  5.4 0.0 copy-start.4
  5.4 0.9 copy-done.4
  6.3 0.0 copy-start.5
  6.3 0.7 copy-done.5
  7.0 0.0 copy-start.6
  7.0 0.7 copy-done.6
  7.8 87.3 %shard_map.110 = (f32[4,4,8,512]{3,2,1,0:T(8,128)S(1)}, f32[4,4,8,512]{3,2,1,0:T(8,128)S(1)}, f32[16,8,512]{2,1,0:T(8,128)S(1)}, f32[8,512]{1,0:T(8,128)S(1)}, f32[8,512]{1,0:T(8,128)S(1)}) custom-call(bf16[368,4096]{1,0:T(8,128)(2,1)S(1)} %bitcast.12, bf16[368,512]{1,0:T(8,128)(2,1)S(1)} %bitcast.13, f32[4,4,8,512]{3,2,1,0:T(8,128)S(1)} %bitcast.14, ...), custom_call_target="tpu_custom_call" | custom-call | tf_op jit(solution)/shard_map/pallas_call | solution.py:427
  95.0 0.7 copy.17
  95.8 0.7 copy.18
  96.5 0.7 copy.19
  97.2 0.6 copy.20
  97.8 0.6 copy.21
Async XLA Ops:
  0.6 1.9 %copy-start = (bf16[1,368,4096]{2,1,0:T(8,128)(2,1)S(1)}, bf16[1,368,4096]{2,1,0:T(8,128)(2,1)}, u32[]{:S(2)}) copy-start(bf16[1,368,4096]{2,1,0:T(8,128)(2,1)} %param.7) | copy-start | bytes 9043972
  2.5 1.0 %copy-start.1 = (bf16[1,368,512]{2,1,0:T(8,128)(2,1)S(1)}, bf16[1,368,512]{2,1,0:T(8,128)(2,1)}, u32[]{:S(2)}) copy-start(bf16[1,368,512]{2,1,0:T(8,128)(2,1)} %param.8) | copy-start | bytes 1130500
  3.5 0.9 copy-start.2
  4.4 0.9 copy-start.3
  5.4 0.9 copy-start.4
  6.3 0.7 copy-start.5
  7.0 0.7 copy-start.6

commit v2 on v1

--- a/solution.py
+++ b/solution.py
@@ -302,21 +302,20 @@
         axis = axis_of(0, half)
         group = wrap(position(axis) + offset)
 
-        def one(e, carry):
-            k = group * SIDE + e if half == 0 else e * SIDE + group
-            product = lax.dot_general(
-                actb[k],
-                kgb[:, half * half_cols : (half + 1) * half_cols],
-                (((0,), (0,)), ((), ())),
-                preferred_element_type=jnp.float32,
-            )
+        blocks = [
+            actb[group * SIDE + e if half == 0 else e * SIDE + group] for e in range(SIDE)
+        ]
+        product = lax.dot_general(
+            jnp.concatenate(blocks, axis=1),
+            kgb[:, half * half_cols : (half + 1) * half_cols],
+            (((0,), (0,)), ((), ())),
+            preferred_element_type=jnp.float32,
+        )
+        for e in range(SIDE):
             for s in range(STAGES):
                 for j in range(groups):
-                    row = (j * STAGES + s) * 8
+                    row = e * islands * 8 + (j * STAGES + s) * 8
                     part[s, half, group * SIDE + e, j * 8 : (j + 1) * 8, :] = product[row : row + 8, :]
-            return carry
-
-        lax.fori_loop(0, SIDE, one, 0)
 
     loads[0].wait()
     sibling_kg.wait_recv()
@@ -335,48 +334,53 @@
         send(0, 0, half, 1, 1).start()
     for half in (0, 1):
         multiply(half, 0)
+
+    def firsts(s):
+        for half in (0, 1):
+            first(s, 0, half)
+
+    def seconds(s):
+        for half in (0, 1):
+            second(s, 0, half)
+
+    def relays(s, phase):
+        for half in (0, 1):
+            relay(s, phase, half)
+
+    def collects(s):
+        for half in (0, 1):
+            collect(s, 0, half)
+            first(s, 1, half)
+            second(s, 1, half)
+
+    firsts(1)
+    seconds(1)
+    relays(0, 0)
+    firsts(2)
+    relays(1, 0)
+    seconds(2)
+    collects(0)
+    firsts(3)
+    relays(2, 0)
+    seconds(3)
+    collects(1)
+    relays(0, 1)
+    relays(3, 0)
     for copy in loads[1:]:
         copy.wait()
-
-    def stage(t, carry):
-        @pl.when(t < STAGES)
-        def _():
-            for half in (0, 1):
-                relay(t, 0, half)
-
-        @pl.when(t + 1 < STAGES)
-        def _():
-            for half in (0, 1):
-                first(t + 1, 0, half)
-
-        @pl.when(t >= 1)
-        def _():
-            inner_step(t - 1)
-
-        @pl.when(t < STAGES)
-        def _():
-            for half in (0, 1):
-                collect(t, 0, half)
-                first(t, 1, half)
-                second(t, 1, half)
-
-        @pl.when(t + 1 < STAGES)
-        def _():
-            for half in (0, 1):
-                second(t + 1, 0, half)
-
-        @pl.when(t < STAGES)
-        def _():
-            for half in (0, 1):
-                relay(t, 1, half)
-
-        @pl.when(t >= 1)
-        def _():
-            outer_step(t - 1)
-
-        return carry
-
-    lax.fori_loop(0, STAGES + 1, stage, 0)
+    inner_step(0)
+    collects(2)
+    relays(1, 1)
+    collects(3)
+    relays(2, 1)
+    inner_step(1)
+    relays(3, 1)
+    inner_step(2)
+    outer_step(0)
+    inner_step(3)
+    outer_step(1)
+    outer_step(2)
+    outer_step(3)
 
     sibling_kg.wait_send()
     for visits in (far_x, far_y, rest):
@@ -403,6 +407,15 @@
 
     lax.fori_loop(1, islands, last, 0)
     for copy in save_outer:
+        copy.wait()
+
+
+def place(*refs):
+    sem = refs[-1]
+    copies = [pltpu.make_async_copy(refs[i], refs[5 + i], sem.at[i]) for i in range(5)]
+    for copy in copies:
+        copy.start()
+    for copy in copies:
         copy.wait()
 
 
@@ -424,7 +437,7 @@
     def kernel(*refs):
         window(islands, *refs)
 
-    m_next, v_next, refreshed, new_anchor, moment = pl.pallas_call(
+    results = pl.pallas_call(
         kernel,
         out_shape=(
             jax.ShapeDtypeStruct(state, f32),
@@ -465,17 +478,25 @@
             dma((3, STAGES)),
         ],
         compiler_params=pltpu.CompilerParams(
-            collective_id=0, has_side_effects=True, vmem_limit_bytes=48 * 1024 * 1024
+            collective_id=0, has_side_effects=True, vmem_limit_bytes=40 * 1024 * 1024
         ),
     )(
-        activations[0],
+        *(pltpu.with_memory_space_constraint(r, pltpu.MemorySpace.HBM) for r in (activations[0],
         key_grad[0],
         island_weight.reshape(state),
         adam_m.reshape(state),
         adam_v.reshape(state),
         anchor[0],
-        outer_momentum[0],
+        outer_momentum[0])),
     )
+    m_next, v_next, refreshed, new_anchor, moment = pl.pallas_call(
+        place,
+        out_shape=tuple(jax.ShapeDtypeStruct(r.shape, f32) for r in results),
+        in_specs=[hbm] * 5,
+        out_specs=(hbm,) * 5,
+        scratch_shapes=[dma((5,))],
+        compiler_params=pltpu.CompilerParams(vmem_limit_bytes=1024 * 1024),
+    )(*results)
     return (
         m_next.reshape(island_weight.shape),
         v_next.reshape(island_weight.shape),

time: 98.8 us -> 80.9 us (0.82)
  the two profiles are of different devices: /device:TPU:8 before, /device:TPU:2 now
where the time goes in v2:
time: 80.9 us; the launch traced here: 80.8 us
  Pallas kernels  80.2 us (99%)
    pallas_call x1, Pallas kernels, shards(): pl.pallas_call(kernel, out_shape=(jax.ShapeDtypeStruct(state, f32), jax.S...  79.2 us

profile of v2, /device:TPU:2, one launch (start us, length us, event | category | flops | bytes accessed | tf_op | source)
XLA Modules:
  0.0 80.8 jit_solution(3152243123485328705)
XLA Ops:
  0.6 79.2 %shard_map.110 = (f32[4,4,8,512]{3,2,1,0:T(8,128)S(1)}, f32[4,4,8,512]{3,2,1,0:T(8,128)S(1)}, f32[16,8,512]{2,1,0:T(8,128)S(1)}, f32[8,512]{1,0:T(8,128)S(1)}, f32[8,512]{1,0:T(8,128)S(1)}) custom-call(bf16[368,4096]{1,0:T(8,128)(2,1)} %bitcast.12, bf16[368,512]{1,0:T(8,128)(2,1)} %bitcast.13, f32[4,4,8,512]{3,2,1,0:T(8,128)} %bitcast.14, ...), custom_call_target="tpu_custom_call" | custom-call | tf_op jit(solution)/shard_map/pallas_call | solution.py:440
  79.9 0.9 %shard_map.111 = (f32[4,4,8,512]{3,2,1,0:T(8,128)}, f32[4,4,8,512]{3,2,1,0:T(8,128)}, f32[16,8,512]{2,1,0:T(8,128)}, f32[8,512]{1,0:T(8,128)}, f32[8,512]{1,0:T(8,128)}) custom-call(f32[4,4,8,512]{3,2,1,0:T(8,128)S(1)} %get-tuple-element.15.refs_0_, f32[4,4,8,512]{3,2,1,0:T(8,128)S(1)} %get-tuple-element.16.refs_1_, ...), custom_call_target="tpu_custom_call" | custom-call | tf_op jit(solution)/shard_map/pallas_call | solution.py:492

commit v3 on v2

--- a/solution.py
+++ b/solution.py
@@ -15,6 +15,7 @@
 
 SIDE = 4
 STAGES = 4
+PAIR = 2
 MESH = pl.DeviceIdType.MESH
 
 
@@ -22,7 +23,7 @@
     islands,
     act, kg, weight, adam_m, adam_v, anchor, momentum,
     m_out, v_out, w_out, a_out, o_out,
-    actb, kgb, part, got1, got2, wb, mb, vb, mnb, vnb, step_b, zgot, ab, ob, anb, onb,
+    actb, kgb, part, got1, got2, wb, mb, vb, mnb, vnb, step_b, zgot, ab, ob, anb, onb, fresh,
     load_sem, act_sem, sib_send, sib_recv, xy_send, xy_recv, zr_send, zr_recv, ag_send, ag_recv, out_sem,
 ):
     me = lax.axis_index("island")
@@ -32,7 +33,7 @@
     x = lax.div(chip, SIDE)
     y = lax.rem(chip, SIDE)
     tokens = kg.shape[0]
-    groups = islands // STAGES
+    groups = islands // PAIR
     half_cols = kgb.shape[1] // 2
     sibling = flat + 1 - 2 * core
 
@@ -197,74 +198,74 @@
             )
 
     def share_send(s, j):
-        owner = STAGES * j + s
+        chunk, parity = s // PAIR, s % PAIR
+        owner = PAIR * j + parity
         return pltpu.make_async_remote_copy(
             src_ref=step_b.at[s, j],
-            dst_ref=zgot.at[me],
-            send_sem=zr_send.at[owner],
-            recv_sem=zr_recv.at[me],
+            dst_ref=zgot.at[chunk, me],
+            send_sem=zr_send.at[chunk, owner],
+            recv_sem=zr_recv.at[chunk, me],
             device_id={"island": owner},
             device_id_type=MESH,
         )
 
-    def share_from(source):
+    def share_from(chunk, source):
         return pltpu.make_async_remote_copy(
             src_ref=step_b.at[0, 0],
-            dst_ref=zgot.at[source],
-            send_sem=zr_send.at[source],
-            recv_sem=zr_recv.at[source],
+            dst_ref=zgot.at[chunk, source],
+            send_sem=zr_send.at[chunk, source],
+            recv_sem=zr_recv.at[chunk, source],
             device_id={"island": source},
             device_id_type=MESH,
         )
 
-    def fresh_send(owner, target):
+    def fresh_send(chunk, owner, target):
         return pltpu.make_async_remote_copy(
-            src_ref=anb,
-            dst_ref=w_out.at[owner],
-            send_sem=ag_send.at[target],
-            recv_sem=ag_recv.at[owner],
+            src_ref=fresh.at[chunk],
+            dst_ref=w_out.at[chunk, owner],
+            send_sem=ag_send.at[chunk, target],
+            recv_sem=ag_recv.at[chunk, owner],
             device_id={"island": target},
             device_id_type=MESH,
         )
 
-    def save_moments(s):
-        return (
-            pltpu.make_async_copy(mnb.at[:, s], m_out.at[:, s], out_sem.at[0, s]),
-            pltpu.make_async_copy(vnb.at[:, s], v_out.at[:, s], out_sem.at[1, s]),
-        )
-
+    save_moments = (
+        pltpu.make_async_copy(mnb, m_out, out_sem.at[0]),
+        pltpu.make_async_copy(vnb, v_out, out_sem.at[1]),
+    )
     save_outer = (
-        pltpu.make_async_copy(anb, a_out, out_sem.at[2, 0]),
-        pltpu.make_async_copy(onb, o_out, out_sem.at[2, 1]),
-        pltpu.make_async_copy(anb, w_out.at[me], out_sem.at[2, 2]),
+        pltpu.make_async_copy(anb, a_out, out_sem.at[2]),
+        pltpu.make_async_copy(onb, o_out, out_sem.at[3]),
+        pltpu.make_async_copy(fresh, w_out.at[:, me], out_sem.at[4]),
     )
 
+    def columns(chunk, half):
+        return slice(half * half_cols + chunk * 128, half * half_cols + (chunk + 1) * 128)
+
     def inner_step(s):
+        chunk, parity = s // PAIR, s % PAIR
         for half in (0, 1):
             arrived(s, 1, half)
             pos = position(axis_of(1, half))
-            cols = slice(half * half_cols, (half + 1) * half_cols)
+            cols = columns(chunk, half)
             for section in (0, 1):
                 js = slice(section * groups // 2, (section + 1) * groups // 2)
-                shape = (groups // 2, 8, half_cols)
                 grad = (
                     piece(s, 1, half, pos, section)[...]
                     + landing(s, 1, half, section, 2)[...]
                     + landing(s, 1, half, 1 - section, 1)[...]
-                ).reshape(shape)
-                m_next = beta_first * mb[js, s, :, cols] + (1.0 - beta_first) * grad
-                v_next = beta_second * vb[js, s, :, cols] + (1.0 - beta_second) * grad * grad
-                old = wb[js, s, :, cols]
-                mnb[js, s, :, cols] = m_next
-                vnb[js, s, :, cols] = v_next
-                step_b[s, js, :, cols] = old - inner_rate * (
+                ).reshape(groups // 2, 8, 128)
+                m_next = beta_first * mb[js, parity, :, cols] + (1.0 - beta_first) * grad
+                v_next = beta_second * vb[js, parity, :, cols] + (1.0 - beta_second) * grad * grad
+                old = wb[js, parity, :, cols]
+                mnb[js, parity, :, cols] = m_next
+                vnb[js, parity, :, cols] = v_next
+                step_b[s, js, half] = old - inner_rate * (
                     m_next / (jnp.sqrt(v_next) + epsilon) + decay_rate * old
                 )
-        for copy in save_moments(s):
-            copy.start()
 
         def one(j, carry):
-            @pl.when(STAGES * j + s != me)
+            @pl.when(PAIR * j + parity != me)
             def _():
                 share_send(s, j).start()
 
@@ -273,26 +274,31 @@
         lax.fori_loop(0, groups, one, 0)
 
     def outer_step(s):
-        @pl.when(lax.rem(me, STAGES) == s)
+        chunk, parity = s // PAIR, s % PAIR
+
+        @pl.when(lax.rem(me, PAIR) == parity)
         def _():
             def add(d, total):
                 source = lax.rem(me + d, islands)
-                share_from(source).wait_recv()
-                return total + zgot[source]
-
-            total = lax.fori_loop(1, islands, add, step_b[s, lax.div(me, STAGES)])
-            shift = ab[...] - total / float(islands)
-            moment = outer_beta * ob[...] + shift
-            anb[...] = ab[...] - outer_rate * (shift + outer_beta * moment)
-            onb[...] = moment
+                share_from(chunk, source).wait_recv()
+                return total + zgot[chunk, source]
+
+            total = lax.fori_loop(1, islands, add, step_b[s, lax.div(me, PAIR)])
+            for half in (0, 1):
+                cols = columns(chunk, half)
+                old = ab[:, cols]
+                shift = old - total[half] / float(islands)
+                moment = outer_beta * ob[:, cols] + shift
+                new = old - outer_rate * (shift + outer_beta * moment)
+                fresh[chunk, half] = new
+                anb[:, cols] = new
+                onb[:, cols] = moment
 
             def one(d, carry):
-                fresh_send(me, lax.rem(me + d, islands)).start()
+                fresh_send(chunk, me, lax.rem(me + d, islands)).start()
                 return carry
 
             lax.fori_loop(1, islands, one, 0)
-            for copy in save_outer:
-                copy.start()
 
     def wait_block(k):
         own_block(k).wait()
@@ -313,9 +319,12 @@
         )
         for e in range(SIDE):
             for s in range(STAGES):
+                chunk, parity = s // PAIR, s % PAIR
                 for j in range(groups):
-                    row = e * islands * 8 + (j * STAGES + s) * 8
-                    part[s, half, group * SIDE + e, j * 8 : (j + 1) * 8, :] = product[row : row + 8, :]
+                    row = (e * islands + PAIR * j + parity) * 8
+                    part[s, half, group * SIDE + e, j * 8 : (j + 1) * 8, :] = product[
+                        row : row + 8, chunk * 128 : (chunk + 1) * 128
+                    ]
 
     loads[0].wait()
     sibling_kg.wait_recv()
@@ -362,25 +371,27 @@
     collects(0)
     firsts(3)
     relays(2, 0)
-    seconds(3)
     collects(1)
     relays(0, 1)
+    seconds(3)
     relays(3, 0)
+    collects(2)
+    relays(1, 1)
     for copy in loads[1:]:
         copy.wait()
     inner_step(0)
-    collects(2)
-    relays(1, 1)
     collects(3)
     relays(2, 1)
     inner_step(1)
     relays(3, 1)
     inner_step(2)
-    outer_step(0)
     inner_step(3)
-    outer_step(1)
-    outer_step(2)
-    outer_step(3)
+    for copy in save_moments:
+        copy.start()
+    for s in range(STAGES):
+        outer_step(s)
+    for copy in save_outer:
+        copy.start()
 
     sibling_kg.wait_send()
     for visits in (far_x, far_y, rest):
@@ -392,27 +403,30 @@
                 for direction in (0, 1):
                     for message in (0, 1, 2):
                         send(s, phase, half, direction, message).wait_send()
-        for copy in save_moments(s):
-            copy.wait()
         return carry
 
     lax.fori_loop(0, STAGES, finish, 0)
 
     def last(d, carry):
         other = lax.rem(me + d, islands)
-        fresh_send(other, me).wait_recv()
-        share_from(other).wait_send()
-        fresh_send(me, other).wait_send()
+        for chunk in (0, 1):
+            fresh_send(chunk, other, me).wait_recv()
+            share_from(chunk, other).wait_send()
+            fresh_send(chunk, me, other).wait_send()
         return carry
 
     lax.fori_loop(1, islands, last, 0)
-    for copy in save_outer:
+    for copy in save_moments + save_outer:
         copy.wait()
 
 
-def place(*refs):
-    sem = refs[-1]
-    copies = [pltpu.make_async_copy(refs[i], refs[5 + i], sem.at[i]) for i in range(5)]
+def place(m, v, w, a, o, m_out, v_out, w_out, a_out, o_out, sem):
+    pairs = [(m, m_out), (v, v_out), (a, a_out), (o, o_out)]
+    for half in (0, 1):
+        for chunk in (0, 1):
+            start = (2 * half + chunk) * 128
+            pairs.append((w.at[chunk, :, half], w_out.at[:, :, start : start + 128]))
+    copies = [pltpu.make_async_copy(old, new, sem.at[i]) for i, (old, new) in enumerate(pairs)]
     for copy in copies:
         copy.start()
     for copy in copies:
@@ -424,15 +438,15 @@
     columns = key_grad.shape[2]
     rows = island_weight.shape[1]
     islands = lax.axis_size("island")
-    groups = islands // STAGES
+    groups = islands // PAIR
     share = rows // islands
-    half_cols = columns // 2
     blocks = SIDE * SIDE
     f32 = jnp.float32
-    state = (groups, STAGES, share, columns)
+    state = (groups, PAIR, share, columns)
     hbm = pl.BlockSpec(memory_space=pl.ANY)
     dma = pltpu.SemaphoreType.DMA
-    stage_rows = rows // STAGES
+    stage_rows = rows // PAIR
+    tiles = (2, share, 128)
 
     def kernel(*refs):
         window(islands, *refs)
@@ -442,7 +456,7 @@
         out_shape=(
             jax.ShapeDtypeStruct(state, f32),
             jax.ShapeDtypeStruct(state, f32),
-            jax.ShapeDtypeStruct((islands, share, columns), f32),
+            jax.ShapeDtypeStruct((2, islands) + tiles, f32),
             jax.ShapeDtypeStruct((share, columns), f32),
             jax.ShapeDtypeStruct((share, columns), f32),
         ),
@@ -451,31 +465,32 @@
         scratch_shapes=[
             pltpu.VMEM((blocks, 2 * tokens, features // (2 * blocks)), jnp.bfloat16),
             pltpu.VMEM((2 * tokens, columns), jnp.bfloat16),
-            pltpu.VMEM((STAGES, 2, blocks, stage_rows, half_cols), f32),
-            pltpu.VMEM((STAGES, 2, 2, 3, 2, stage_rows, half_cols), f32),
-            pltpu.VMEM((STAGES, 2, 2, 3, stage_rows // 2, half_cols), f32),
+            pltpu.VMEM((STAGES, 2, blocks, stage_rows, 128), f32),
+            pltpu.VMEM((STAGES, 2, 2, 3, 2, stage_rows, 128), f32),
+            pltpu.VMEM((STAGES, 2, 2, 3, stage_rows // 2, 128), f32),
             pltpu.VMEM(state, f32),
             pltpu.VMEM(state, f32),
             pltpu.VMEM(state, f32),
             pltpu.VMEM(state, f32),
             pltpu.VMEM(state, f32),
-            pltpu.VMEM((STAGES, groups, share, columns), f32),
-            pltpu.VMEM((islands, share, columns), f32),
+            pltpu.VMEM((STAGES, groups) + tiles, f32),
+            pltpu.VMEM((2, islands) + tiles, f32),
             pltpu.VMEM((share, columns), f32),
             pltpu.VMEM((share, columns), f32),
             pltpu.VMEM((share, columns), f32),
             pltpu.VMEM((share, columns), f32),
+            pltpu.VMEM((2,) + tiles, f32),
             dma((6,)),
             dma((blocks,)),
             dma((blocks + 1,)),
             dma((blocks + 1,)),
             dma((STAGES, 2, 2, 2, 3)),
             dma((STAGES, 2, 2, 2, 3)),
-            dma((islands,)),
-            dma((islands,)),
-            dma((islands,)),
-            dma((islands,)),
-            dma((3, STAGES)),
+            dma((2, islands)),
+            dma((2, islands)),
+            dma((2, islands)),
+            dma((2, islands)),
+            dma((5,)),
         ],
         compiler_params=pltpu.CompilerParams(
             collective_id=0, has_side_effects=True, vmem_limit_bytes=40 * 1024 * 1024
@@ -491,10 +506,13 @@
     )
     m_next, v_next, refreshed, new_anchor, moment = pl.pallas_call(
         place,
-        out_shape=tuple(jax.ShapeDtypeStruct(r.shape, f32) for r in results),
+        out_shape=tuple(
+            jax.ShapeDtypeStruct(shape, f32)
+            for shape in (state, state, (islands, share, columns), (share, columns), (share, columns))
+        ),
         in_specs=[hbm] * 5,
         out_specs=(hbm,) * 5,
-        scratch_shapes=[dma((5,))],
+        scratch_shapes=[dma((8,))],
         compiler_params=pltpu.CompilerParams(vmem_limit_bytes=1024 * 1024),
     )(*results)
     return (

time: 80.9 us -> 73.7 us (0.911)
  Pallas kernels: 80.2 us -> 72.9 us
    pallas_call x1, Pallas kernels: 79.2 us -> 71.9 us  [shards(): pl.pallas_call(kernel, out_shape=(jax.ShapeDtypeStruct(state, f32), jax.S...]
where the time goes in v3:
time: 73.7 us; the launch traced here: 73.5 us
  Pallas kernels  72.9 us (99%)
    pallas_call x1, Pallas kernels, shards(): pl.pallas_call(kernel, out_shape=(jax.ShapeDtypeStruct(state, f32), jax.S...  71.9 us

profile of v3, /device:TPU:2, one launch (start us, length us, event | category | flops | bytes accessed | tf_op | source)
XLA Modules:
  0.0 73.5 jit_solution(13756120809839225437)
XLA Ops:
  0.6 71.9 %shard_map.110 = (f32[8,2,8,512]{3,2,1,0:T(8,128)S(1)}, f32[8,2,8,512]{3,2,1,0:T(8,128)S(1)}, f32[2,16,2,8,128]{4,3,2,1,0:T(8,128)S(1)}, f32[8,512]{1,0:T(8,128)S(1)}, f32[8,512]{1,0:T(8,128)S(1)}) custom-call(bf16[368,4096]{1,0:T(8,128)(2,1)} %bitcast.12, bf16[368,512]{1,0:T(8,128)(2,1)} %bitcast.13, f32[8,2,8,512]{3,2,1,0:T(8,128)} %bitcast.14, ...), custom_call_target="tpu_custom_call" | custom-call | tf_op jit(solution)/shard_map/pallas_call | solution.py:454
  72.6 0.9 %shard_map.111 = (f32[8,2,8,512]{3,2,1,0:T(8,128)}, f32[8,2,8,512]{3,2,1,0:T(8,128)}, f32[16,8,512]{2,1,0:T(8,128)}, f32[8,512]{1,0:T(8,128)}, f32[8,512]{1,0:T(8,128)}) custom-call(f32[8,2,8,512]{3,2,1,0:T(8,128)S(1)} %get-tuple-element.15.m, f32[8,2,8,512]{3,2,1,0:T(8,128)S(1)} %get-tuple-element.16.v, f32[2,16,2,8,128]{4,3,2,1,0:T(8,128)S(1)} %get-tuple-element.17.w, ...), custom_call_target="tpu_custom_call" | custom-call | tf_op jit(solution)/shard_map/pallas_call | solution.py:507

commit v4 on v3

--- a/solution.py
+++ b/solution.py
@@ -14,8 +14,8 @@
 outer_rate = 0.7
 
 SIDE = 4
-STAGES = 4
 PAIR = 2
+STAGES = 2 * PAIR
 MESH = pl.DeviceIdType.MESH
 
 
@@ -24,7 +24,7 @@
     act, kg, weight, adam_m, adam_v, anchor, momentum,
     m_out, v_out, w_out, a_out, o_out,
     actb, kgb, part, got1, got2, wb, mb, vb, mnb, vnb, step_b, zgot, ab, ob, anb, onb, fresh,
-    load_sem, act_sem, sib_send, sib_recv, xy_send, xy_recv, zr_send, zr_recv, ag_send, ag_recv, out_sem,
+    load_sem, act_sem, sib_send, sib_recv, xy_send, xy_relay, xy_last, zr_send, zr_recv, ag_send, ag_recv, out_sem,
 ):
     me = lax.axis_index("island")
     flat = lax.axis_index("fsdp")
@@ -69,14 +69,16 @@
             device_id_type=MESH,
         )
 
-    sibling_kg = pltpu.make_async_remote_copy(
-        src_ref=kg,
-        dst_ref=kgb.at[pl.ds(tokens, tokens)],
-        send_sem=sib_send.at[SIDE * SIDE],
-        recv_sem=sib_recv.at[SIDE * SIDE],
-        device_id={"fsdp": sibling},
-        device_id_type=MESH,
-    )
+    def sibling_kg(half):
+        cols = slice(half * half_cols, (half + 1) * half_cols)
+        return pltpu.make_async_remote_copy(
+            src_ref=kg.at[:, cols],
+            dst_ref=kgb.at[pl.ds(tokens, tokens), cols],
+            send_sem=sib_send.at[SIDE * SIDE + half],
+            recv_sem=sib_recv.at[SIDE * SIDE + half],
+            device_id={"fsdp": sibling},
+            device_id_type=MESH,
+        )
 
     def far_x(visit):
         def one(e, carry):
@@ -98,12 +100,6 @@
             return carry
 
         lax.fori_loop(0, 9, one, 0)
-
-    loads[0].start()
-    for visits in (far_x, far_y, rest):
-        visits(lambda k: own_block(k).start())
-    for copy in loads[1:]:
-        copy.start()
 
     barrier = pltpu.get_barrier_semaphore()
     for peer in (
@@ -124,9 +120,18 @@
     lax.fori_loop(1, islands, greet, 0)
     pl.semaphore_wait(barrier, 5 + islands - 1)
 
-    sibling_kg.start()
-    for visits in (far_x, far_y, rest):
-        visits(lambda k: sibling_block(k).start())
+    def both(k):
+        sibling_block(k).start()
+        own_block(k).start()
+
+    sibling_kg(0).start()
+    loads[0].start()
+    far_x(both)
+    sibling_kg(1).start()
+    far_y(both)
+    rest(both)
+    for copy in loads[1:]:
+        copy.start()
 
     def neighbour(axis, direction):
         sign = 1 - 2 * direction
@@ -160,8 +165,10 @@
         return pltpu.make_async_remote_copy(
             src_ref=piece(s, phase, half, group, section),
             dst_ref=landing(s, phase, half, direction, message),
-            send_sem=xy_send.at[s, phase, half, direction, message],
-            recv_sem=xy_recv.at[s, phase, half, direction, message],
+            send_sem=xy_send.at[s, phase],
+            recv_sem=(
+                xy_relay.at[s, phase, half, direction] if message == 0 else xy_last.at[s, phase, half]
+            ),
             device_id={"fsdp": neighbour(axis, direction)},
             device_id_type=MESH,
         )
@@ -183,9 +190,9 @@
             send(s, phase, half, direction, 2).start()
 
     def arrived(s, phase, half):
-        for direction in (0, 1):
-            for message in (1, 2):
-                send(s, phase, half, direction, message).wait_recv()
+        buffer = got1 if phase == 0 else got2
+        landed = buffer.at[s, half, :, pl.ds(1, 2)]
+        pltpu.make_async_copy(landed, landed, xy_last.at[s, phase, half]).wait()
 
     def collect(s, phase, half):
         arrived(s, phase, half)
@@ -203,28 +210,22 @@
         return pltpu.make_async_remote_copy(
             src_ref=step_b.at[s, j],
             dst_ref=zgot.at[chunk, me],
-            send_sem=zr_send.at[chunk, owner],
-            recv_sem=zr_recv.at[chunk, me],
+            send_sem=zr_send.at[chunk],
+            recv_sem=zr_recv.at[chunk],
             device_id={"island": owner},
             device_id_type=MESH,
         )
 
-    def share_from(chunk, source):
-        return pltpu.make_async_remote_copy(
-            src_ref=step_b.at[0, 0],
-            dst_ref=zgot.at[chunk, source],
-            send_sem=zr_send.at[chunk, source],
-            recv_sem=zr_recv.at[chunk, source],
-            device_id={"island": source},
-            device_id_type=MESH,
-        )
+    def all_of(chunk, sem):
+        others = zgot.at[chunk, pl.ds(0, islands - 1)]
+        return pltpu.make_async_copy(others, others, sem.at[chunk])
 
     def fresh_send(chunk, owner, target):
         return pltpu.make_async_remote_copy(
             src_ref=fresh.at[chunk],
             dst_ref=w_out.at[chunk, owner],
-            send_sem=ag_send.at[chunk, target],
-            recv_sem=ag_recv.at[chunk, owner],
+            send_sem=ag_send.at[chunk],
+            recv_sem=ag_recv.at[chunk],
             device_id={"island": target},
             device_id_type=MESH,
         )
@@ -278,12 +279,9 @@
 
         @pl.when(lax.rem(me, PAIR) == parity)
         def _():
-            def add(d, total):
-                source = lax.rem(me + d, islands)
-                share_from(chunk, source).wait_recv()
-                return total + zgot[chunk, source]
-
-            total = lax.fori_loop(1, islands, add, step_b[s, lax.div(me, PAIR)])
+            zgot[chunk, me] = step_b[s, lax.div(me, PAIR)]
+            all_of(chunk, zr_recv).wait()
+            total = jnp.sum(zgot[chunk], axis=0)
             for half in (0, 1):
                 cols = columns(chunk, half)
                 old = ab[:, cols]
@@ -326,21 +324,25 @@
                         row : row + 8, chunk * 128 : (chunk + 1) * 128
                     ]
 
+    early_first = (0, 1)
+    early_second = (0, 1)
     loads[0].wait()
-    sibling_kg.wait_recv()
+    sibling_kg(0).wait_recv()
     far_x(wait_block)
     multiply(0, 2)
-    first(0, 0, 0)
+    for s in early_first:
+        first(s, 0, 0)
+    sibling_kg(1).wait_recv()
     far_y(wait_block)
     multiply(1, 2)
-    first(0, 0, 1)
+    for s in early_first:
+        first(s, 0, 1)
     rest(wait_block)
-    for half in (0, 1):
-        multiply(half, 1)
-        send(0, 0, half, 0, 1).start()
-    for half in (0, 1):
-        multiply(half, 3)
-        send(0, 0, half, 1, 1).start()
+    for direction, offset in ((0, 1), (1, 3)):
+        for half in (0, 1):
+            multiply(half, offset)
+            for s in early_second:
+                send(s, 0, half, direction, 1).start()
     for half in (0, 1):
         multiply(half, 0)
 
@@ -352,9 +354,13 @@
         for half in (0, 1):
             second(s, 0, half)
 
-    def relays(s, phase):
-        for half in (0, 1):
-            relay(s, phase, half)
+    def relays_far(s):
+        for half in (0, 1):
+            relay(s, 0, half)
+
+    def relays_near(s):
+        for half in (0, 1):
+            relay(s, 1, half)
 
     def collects(s):
         for half in (0, 1):
@@ -362,60 +368,50 @@
             first(s, 1, half)
             second(s, 1, half)
 
-    firsts(1)
-    seconds(1)
-    relays(0, 0)
+    relays_far(0)
     firsts(2)
-    relays(1, 0)
+    relays_far(1)
     seconds(2)
     collects(0)
     firsts(3)
-    relays(2, 0)
+    relays_far(2)
     collects(1)
-    relays(0, 1)
+    relays_near(0)
     seconds(3)
-    relays(3, 0)
+    relays_far(3)
     collects(2)
-    relays(1, 1)
+    relays_near(1)
     for copy in loads[1:]:
         copy.wait()
     inner_step(0)
     collects(3)
-    relays(2, 1)
+    relays_near(2)
     inner_step(1)
-    relays(3, 1)
+    relays_near(3)
     inner_step(2)
     inner_step(3)
     for copy in save_moments:
         copy.start()
-    for s in range(STAGES):
-        outer_step(s)
+    outer_step(0)
+    outer_step(1)
+    outer_step(2)
+    outer_step(3)
     for copy in save_outer:
         copy.start()
 
-    sibling_kg.wait_send()
+    for half in (0, 1):
+        sibling_kg(half).wait_send()
     for visits in (far_x, far_y, rest):
         visits(lambda k: sibling_block(k).wait_send())
 
-    def finish(s, carry):
-        for phase in (0, 1):
-            for half in (0, 1):
-                for direction in (0, 1):
-                    for message in (0, 1, 2):
-                        send(s, phase, half, direction, message).wait_send()
-        return carry
-
-    lax.fori_loop(0, STAGES, finish, 0)
-
-    def last(d, carry):
-        other = lax.rem(me + d, islands)
-        for chunk in (0, 1):
-            fresh_send(chunk, other, me).wait_recv()
-            share_from(chunk, other).wait_send()
-            fresh_send(chunk, me, other).wait_send()
-        return carry
-
-    lax.fori_loop(1, islands, last, 0)
+    for s in range(STAGES):
+        for phase, buffer in ((0, got1), (1, got2)):
+            pltpu.make_async_copy(buffer.at[s], buffer.at[s], xy_send.at[s, phase]).wait()
+    for chunk in (0, 1):
+        all_of(chunk, zr_send).wait()
+        all_of(chunk, ag_recv).wait()
+    for chunk in (0, 1):
+        all_of(chunk, ag_send).wait()
     for copy in save_moments + save_outer:
         copy.wait()
 
@@ -482,14 +478,15 @@
             pltpu.VMEM((2,) + tiles, f32),
             dma((6,)),
             dma((blocks,)),
-            dma((blocks + 1,)),
-            dma((blocks + 1,)),
-            dma((STAGES, 2, 2, 2, 3)),
-            dma((STAGES, 2, 2, 2, 3)),
-            dma((2, islands)),
-            dma((2, islands)),
-            dma((2, islands)),
-            dma((2, islands)),
+            dma((blocks + 2,)),
+            dma((blocks + 2,)),
+            dma((STAGES, 2)),
+            dma((STAGES, 2, 2, 2)),
+            dma((STAGES, 2, 2)),
+            dma((2,)),
+            dma((2,)),
+            dma((2,)),
+            dma((2,)),
             dma((5,)),
         ],
         compiler_params=pltpu.CompilerParams(

time: 73.7 us -> 69.8 us (0.947)
  Pallas kernels: 72.9 us -> 69 us
    pallas_call x1, Pallas kernels: 71.9 us -> 68 us  [shards(): pl.pallas_call(kernel, out_shape=(jax.ShapeDtypeStruct(state, f32), jax.S...]
where the time goes in v4:
time: 69.8 us; the launch traced here: 69.6 us
  Pallas kernels  69 us (99%)
    pallas_call x1, Pallas kernels, shards(): pl.pallas_call(kernel, out_shape=(jax.ShapeDtypeStruct(state, f32), jax.S...  68 us

profile of v4, /device:TPU:2, one launch (start us, length us, event | category | flops | bytes accessed | tf_op | source)
XLA Modules:
  0.0 69.6 jit_solution(8551190615639760447)
XLA Ops:
  0.6 68.0 %shard_map.110 = (f32[8,2,8,512]{3,2,1,0:T(8,128)S(1)}, f32[8,2,8,512]{3,2,1,0:T(8,128)S(1)}, f32[2,16,2,8,128]{4,3,2,1,0:T(8,128)S(1)}, f32[8,512]{1,0:T(8,128)S(1)}, f32[8,512]{1,0:T(8,128)S(1)}) custom-call(bf16[368,4096]{1,0:T(8,128)(2,1)} %bitcast.12, bf16[368,512]{1,0:T(8,128)(2,1)} %bitcast.13, f32[8,2,8,512]{3,2,1,0:T(8,128)} %bitcast.14, ...), custom_call_target="tpu_custom_call" | custom-call | tf_op jit(solution)/shard_map/pallas_call | solution.py:450
  68.7 0.9 %shard_map.111 = (f32[8,2,8,512]{3,2,1,0:T(8,128)}, f32[8,2,8,512]{3,2,1,0:T(8,128)}, f32[16,8,512]{2,1,0:T(8,128)}, f32[8,512]{1,0:T(8,128)}, f32[8,512]{1,0:T(8,128)}) custom-call(f32[8,2,8,512]{3,2,1,0:T(8,128)S(1)} %get-tuple-element.15.m, f32[8,2,8,512]{3,2,1,0:T(8,128)S(1)} %get-tuple-element.16.v, f32[2,16,2,8,128]{4,3,2,1,0:T(8,128)S(1)} %get-tuple-element.17.w, ...), custom_call_target="tpu_custom_call" | custom-call | tf_op jit(solution)/shard_map/pallas_call | solution.py:504

commit v5 on v4

--- a/solution.py
+++ b/solution.py
@@ -265,10 +265,16 @@
                     m_next / (jnp.sqrt(v_next) + epsilon) + decay_rate * old
                 )
 
-        def one(j, carry):
-            @pl.when(PAIR * j + parity != me)
+        def one(k, carry):
+            sign = 1 - 2 * lax.rem(k, 2)
+            even = 2 * lax.div(k + 1, 2) * sign
+            uneven = lax.rem(k, 2) * k - (1 - lax.rem(k, 2)) * (k + 1)
+            off = lax.rem(me + parity, 2)
+            owner = lax.rem(me + islands // 2 + even + off * (uneven - even) + islands, islands)
+
+            @pl.when(owner != me)
             def _():
-                share_send(s, j).start()
+                share_send(s, lax.div(owner, PAIR)).start()
 
             return carry
 
@@ -292,11 +298,12 @@
                 anb[:, cols] = new
                 onb[:, cols] = moment
 
-            def one(d, carry):
+            def one(k, carry):
+                d = islands // 2 + lax.div(k + 1, 2) * (1 - 2 * lax.rem(k, 2))
                 fresh_send(chunk, me, lax.rem(me + d, islands)).start()
                 return carry
 
-            lax.fori_loop(1, islands, one, 0)
+            lax.fori_loop(0, islands - 1, one, 0)
 
     def wait_block(k):
         own_block(k).wait()

time: 69.8 us -> 68 us (0.974)
  Pallas kernels: 69 us -> 67.2 us
    pallas_call x1, Pallas kernels: 68 us -> 66.2 us  [shards(): pl.pallas_call(kernel, out_shape=(jax.ShapeDtypeStruct(state, f32), jax.S...]
where the time goes in v5:
time: 68 us; the launch traced here: 67.8 us
  Pallas kernels  67.2 us (99%)
    pallas_call x1, Pallas kernels, shards(): pl.pallas_call(kernel, out_shape=(jax.ShapeDtypeStruct(state, f32), jax.S...  66.2 us

profile of v5, /device:TPU:2, one launch (start us, length us, event | category | flops | bytes accessed | tf_op | source)
XLA Modules:
  0.0 67.8 jit_solution(2259221807977167331)
XLA Ops:
  0.6 66.2 %shard_map.110 = (f32[8,2,8,512]{3,2,1,0:T(8,128)S(1)}, f32[8,2,8,512]{3,2,1,0:T(8,128)S(1)}, f32[2,16,2,8,128]{4,3,2,1,0:T(8,128)S(1)}, f32[8,512]{1,0:T(8,128)S(1)}, f32[8,512]{1,0:T(8,128)S(1)}) custom-call(bf16[368,4096]{1,0:T(8,128)(2,1)} %bitcast.12, bf16[368,512]{1,0:T(8,128)(2,1)} %bitcast.13, f32[8,2,8,512]{3,2,1,0:T(8,128)} %bitcast.14, ...), custom_call_target="tpu_custom_call" | custom-call | tf_op jit(solution)/shard_map/pallas_call | solution.py:457
  66.9 0.9 %shard_map.111 = (f32[8,2,8,512]{3,2,1,0:T(8,128)}, f32[8,2,8,512]{3,2,1,0:T(8,128)}, f32[16,8,512]{2,1,0:T(8,128)}, f32[8,512]{1,0:T(8,128)}, f32[8,512]{1,0:T(8,128)}) custom-call(f32[8,2,8,512]{3,2,1,0:T(8,128)S(1)} %get-tuple-element.15.m, f32[8,2,8,512]{3,2,1,0:T(8,128)S(1)} %get-tuple-element.16.v, f32[2,16,2,8,128]{4,3,2,1,0:T(8,128)S(1)} %get-tuple-element.17.w, ...), custom_call_target="tpu_custom_call" | custom-call | tf_op jit(solution)/shard_map/pallas_call | solution.py:511

commit v6 on v4

--- a/solution.py
+++ b/solution.py
@@ -265,14 +265,19 @@
                     m_next / (jnp.sqrt(v_next) + epsilon) + decay_rate * old
                 )
 
-        def one(j, carry):
-            @pl.when(PAIR * j + parity != me)
-            def _():
-                share_send(s, j).start()
-
-            return carry
-
-        lax.fori_loop(0, groups, one, 0)
+        middle, off = islands // 2, lax.rem(me + parity, PAIR)
+        for k in range(groups):
+            even = middle + 2 * ((k + 1) // 2) * (1 - 2 * (k % 2))
+            uneven = middle + (k if k % 2 else -k - 1)
+            owner = lax.rem(me + even + off * (uneven - even), islands)
+            if even == 0:
+
+                @pl.when(off == 1)
+                def _(owner=owner):
+                    share_send(s, lax.div(owner, PAIR)).start()
+
+            else:
+                share_send(s, lax.div(owner, PAIR)).start()
 
     def outer_step(s):
         chunk, parity = s // PAIR, s % PAIR
@@ -292,11 +297,9 @@
                 anb[:, cols] = new
                 onb[:, cols] = moment
 
-            def one(d, carry):
-                fresh_send(chunk, me, lax.rem(me + d, islands)).start()
-                return carry
-
-            lax.fori_loop(1, islands, one, 0)
+            for away in range(islands // 2, 0, -1):
+                for d in sorted({away, islands - away}):
+                    fresh_send(chunk, me, lax.rem(me + d, islands)).start()
 
     def wait_block(k):
         own_block(k).wait()

time: 69.8 us -> 67.9 us (0.973)
  Pallas kernels: 69 us -> 67.2 us
    pallas_call x1, Pallas kernels: 68 us -> 66.2 us  [shards(): pl.pallas_call(kernel, out_shape=(jax.ShapeDtypeStruct(state, f32), jax.S...]
where the time goes in v6:
time: 67.9 us; the launch traced here: 67.8 us
  Pallas kernels  67.2 us (99%)
    pallas_call x1, Pallas kernels, shards(): pl.pallas_call(kernel, out_shape=(jax.ShapeDtypeStruct(state, f32), jax.S...  66.2 us

profile of v6, /device:TPU:2, one launch (start us, length us, event | category | flops | bytes accessed | tf_op | source)
XLA Modules:
  0.0 67.8 jit_solution(14816909317268928773)
XLA Ops:
  0.6 66.2 %shard_map.110 = (f32[8,2,8,512]{3,2,1,0:T(8,128)S(1)}, f32[8,2,8,512]{3,2,1,0:T(8,128)S(1)}, f32[2,16,2,8,128]{4,3,2,1,0:T(8,128)S(1)}, f32[8,512]{1,0:T(8,128)S(1)}, f32[8,512]{1,0:T(8,128)S(1)}) custom-call(bf16[368,4096]{1,0:T(8,128)(2,1)} %bitcast.12, bf16[368,512]{1,0:T(8,128)(2,1)} %bitcast.13, f32[8,2,8,512]{3,2,1,0:T(8,128)} %bitcast.14, ...), custom_call_target="tpu_custom_call" | custom-call | tf_op jit(solution)/shard_map/pallas_call | solution.py:453
  66.8 0.9 %shard_map.111 = (f32[8,2,8,512]{3,2,1,0:T(8,128)}, f32[8,2,8,512]{3,2,1,0:T(8,128)}, f32[16,8,512]{2,1,0:T(8,128)}, f32[8,512]{1,0:T(8,128)}, f32[8,512]{1,0:T(8,128)}) custom-call(f32[8,2,8,512]{3,2,1,0:T(8,128)S(1)} %get-tuple-element.15.m, f32[8,2,8,512]{3,2,1,0:T(8,128)S(1)} %get-tuple-element.16.v, f32[2,16,2,8,128]{4,3,2,1,0:T(8,128)S(1)} %get-tuple-element.17.w, ...), custom_call_target="tpu_custom_call" | custom-call | tf_op jit(solution)/shard_map/pallas_call | solution.py:507
